TPU v7x, 32 devices: a whole 2x2x4 slice. The times are simulated.
32 devices in a mesh: fsdp: 16 (over z, y, x), dp: 2 (over core).
Axes of the slice: x: 2, y: 2, z: 4, core: 2. Of those that a mesh axis runs over, the one named last changes fastest.
Arguments:
- grads: bfloat16 [2, 1024, 28672], P('dp', 'fsdp')
- block_slot: int32 [28], replicated, may hold values from 0 to 31, as said below
- left_stats: float32 [32, 1024, 1024], P('fsdp', 'dp')
- right_stats: float32 [32, 1024, 1024], P('fsdp', 'dp')
- left_root: bfloat16 [32, 1024, 1024], P('fsdp', 'dp')
- right_root: bfloat16 [32, 1024, 1024], P('fsdp', 'dp')
Outputs:
- left_new: float32 [32, 1024, 1024], P('fsdp', 'dp')
- right_new: float32 [32, 1024, 1024], P('fsdp', 'dp')
- update: bfloat16 [1024, 28672], P('fsdp')
Inputs may be any that keep to these rules, and one draw needn't show every extreme that they name: The entries of block_slot are distinct. Block b's statistics and roots sit in slot block_slot[b], which belongs to the fsdp device of index block_slot[b] // 2; slots that no block names are empty and their statistics pass through unchanged.
All inputs are finite; a program needn't handle non-finite values.
Results may differ from a plain program's by a relative error of at most 0.015.
Values may be sent and summed in bfloat16 or wider, within the bound.
A program may use at most 128 MiB of HBM per device.

v0:
```python
import jax
import jax.numpy as jnp
from jax import lax
from jax.sharding import PartitionSpec as P

epsilon = 1e-06


def per_device(grads, block_slot, left_stats, right_stats, left_root, right_root):
    local_rows = grads[0]
    row_dev, col_count = local_rows.shape
    block_size = left_stats.shape[2]
    block_count = col_count // block_size
    slot_count = left_stats.shape[0]
    shared_rows = left_stats.shape[1]
    total_slots = slot_count * lax.axis_size("fsdp")
    slot_ids = jnp.arange(total_slots, dtype=jnp.int32)
    matches = block_slot[None, :] == slot_ids[:, None]
    filled = jnp.any(matches, axis=1)
    source = jnp.sum(
        jnp.where(matches, jnp.arange(block_count, dtype=jnp.int32)[None, :], 0), axis=1
    )
    row_start = lax.axis_index("dp") * shared_rows
    band = local_rows.astype(jnp.float32).reshape(row_dev, block_count, block_size)
    shares = lax.psum_scatter(band.astype(jnp.bfloat16), "dp", scatter_dimension=2, tiled=True)
    outgoing = jnp.where(
        filled[None, :, None], jnp.take(shares, source, axis=1), jnp.zeros((), jnp.bfloat16)
    )
    incoming = lax.all_to_all(outgoing, "fsdp", split_axis=1, concat_axis=0, tiled=True)
    gradient = lax.all_gather(incoming, "dp", axis=2, tiled=True)
    own_rows = lax.dynamic_slice_in_dim(gradient, row_start, shared_rows, 0)
    whole_right = lax.all_gather(right_root, "dp", axis=1, tiled=True)
    left_new = left_stats + jnp.einsum(
        "rjc,kjc->jrk", own_rows, gradient, preferred_element_type=jnp.float32
    )
    columns = lax.dynamic_slice_in_dim(gradient, row_start, shared_rows, 2)
    right_new = right_stats + jnp.einsum(
        "rjc,rjk->jck", columns, gradient, preferred_element_type=jnp.float32
    )
    left_applied = jnp.einsum(
        "jrk,kjc->rjc", left_root, gradient, preferred_element_type=jnp.float32
    ).astype(jnp.bfloat16)
    both_applied = jnp.einsum(
        "rjc,jck->rjk", left_applied, whole_right, preferred_element_type=jnp.float32
    )
    squares = lax.psum(jnp.sum(both_applied * both_applied, axis=(0, 2)), "dp")
    factor = lax.rsqrt(squares / (block_size * block_size) + epsilon)
    scaled = (both_applied * factor[None, :, None]).astype(jnp.bfloat16)
    full_rows = lax.all_gather(scaled, "dp", axis=0, tiled=True)
    returned = lax.all_to_all(full_rows, "fsdp", split_axis=0, concat_axis=1, tiled=True)
    update = jnp.take(returned, block_slot, axis=1).reshape(row_dev, col_count)
    return (left_new, right_new, update)


def solution(mesh):
    in_specs = (
        P("dp", "fsdp", None),
        P(),
        P("fsdp", "dp", None),
        P("fsdp", "dp", None),
        P("fsdp", "dp", None),
        P("fsdp", "dp", None),
    )
    out_specs = (P("fsdp", "dp", None), P("fsdp", "dp", None), P("fsdp", None))
    return jax.shard_map(
        per_device, mesh=mesh, in_specs=in_specs, out_specs=out_specs, check_vma=False
    )
```

profile of v0, /device:TPU:14, one launch (start us, length us, event | category | flops | bytes accessed | tf_op | source)
XLA Modules:
  0.0 272.9 jit_solution(7911280126792472011)
XLA Ops:
  7.2 5.7 %squeeze.3 = bf16[64,28,1024]{2,1,0:T(8,128)(2,1)} reshape(bf16[1,64,28672]{2,1,0:T(8,128)(2,1)} %param.6) | data formatting | bytes 7340032 | tf_op jit(solution)/shard_map/squeeze | solution.py:10
  12.9 6.0 %copy.31 = bf16[64,28,1024]{2,0,1:T(8,128)(2,1)} copy(bf16[64,28,1024]{2,1,0:T(8,128)(2,1)} %squeeze.3) | data formatting | bytes 7340032 | tf_op jit(solution)/shard_map/squeeze | solution.py:10
  19.0 0.7 all-gather.6.cloned.1.call-update
  19.9 0.1 fusion.16
  20.1 12.2 %reduce-scatter.2.cloned.1.call-done = bf16[64,28,512]{2,0,1:T(8,128)(2,1)} async-done(((bf16[64,28,1024]{2,0,1:T(8,128)(2,1)}), bf16[64,28,512]{2,0,1:T(8,128)(2,1)}) %reduce-scatter.2.cloned.1.call-update) | async-done | bytes 1835024 | tf_op jit(solution)/shard_map/reduce_scatter | solution.py:25
  32.3 3.5 %gather_fusion = bf16[32,64,512]{2,1,0:T(8,128)(2,1)} fusion(bf16[64,28,512]{2,0,1:T(8,128)(2,1)} %reduce-scatter.2.cloned.1.call-done, s32[1024]{0:T(1024)S(1)} %pad_clamp_fusion.1), kind=kCustom, calls=%fused_computation | custom fusion | bytes 4194432 | tf_op jit(solution)/shard_map/jit(_take)/gather | solution.py:27
  35.8 1.9 select_bitcast_fusion
  37.7 53.8 %all_to_all.36 = bf16[64,32,512]{2,0,1:T(8,128)(2,1)S(1)} all-to-all(bf16[64,32,512]{2,0,1:T(8,128)(2,1)S(1)} %select_bitcast_fusion), channel_id=1, replica_groups=mesh['fsdp'=16,'dp'=2] {'fsdp'}, dimensions={1} | all-to-all | bytes 4194304 | tf_op jit(solution)/shard_map/all_to_all | solution.py:29
  91.5 1.5 copy.32
  93.1 14.0 %all-gather.4.cloned.1.call-done = bf16[1024,2,1024]{2,0,1:T(8,128)(2,1)} async-done(((bf16[1024,2,512]{2,0,1:T(8,128)(2,1)}), bf16[1024,2,1024]{2,0,1:T(8,128)(2,1)}) %all-gather.4.cloned.1.call-update) | async-done | bytes 4194320 | tf_op jit(solution)/shard_map/all_gather | solution.py:30
  107.0 10.4 %multiply_reduce_fusion = (f32[2]{0:T(128)S(1)}, f32[2,512,1024]{2,1,0:T(8,128)}) fusion(bf16[2,1024,1024]{2,1,0:T(8,128)(2,1)} %all-gather.6.cloned.1.call-done, bf16[1024,2,1024]{2,0,1:T(8,128)(2,1)} %all-gather.4.cloned.1.call-done, bf16[2,512,1024]{2,1,0:T(8,128)(2,1)S(1)} %copy-done), kind=kOutput, calls=%fused_computation.3 | convolution fusion | flops 4298113024 | bytes 14680072 | tf_op jit(solution)/shard_map/rjc,jck->rjk/dot_general | solution.py:43
  117.5 2.6 psum.7
  120.1 4.1 %fusion = bf16[512,2,1024]{2,0,1:T(8,128)(2,1)} fusion(f32[2,512,1024]{2,1,0:T(8,128)} %get-tuple-element.4, f32[2]{0:T(128)S(1)} %add_rsqrt_fusion), kind=kLoop, calls=%fused_computation.5 | loop fusion | flops 2097152 | bytes 6291464 | tf_op jit(solution)/shard_map/convert_element_type | solution.py:48
  124.3 15.0 %all-gather.8.cloned.1.call-done = bf16[1024,2,1024]{2,0,1:T(8,128)(2,1)} async-done(((bf16[512,2,1024]{2,0,1:T(8,128)(2,1)}), bf16[1024,2,1024]{2,0,1:T(8,128)(2,1)}) %all-gather.8.cloned.1.call-update) | async-done | bytes 4194320 | tf_op jit(solution)/shard_map/all_gather | solution.py:49
  139.3 8.5 %copy.36 = bf16[1024,2,1024]{2,1,0:T(2,128)(2,1)} copy(bf16[1024,2,1024]{2,0,1:T(8,128)(2,1)} %all-gather.8.cloned.1.call-done) | data formatting | bytes 8388608 | tf_op jit(solution)/shard_map/all_gather | solution.py:49
  147.7 7.0 %all-to-all-start.1 = ((bf16[1024,2,1024]{2,1,0:T(2,128)(2,1)}), bf16[1024,2,1024]{2,1,0:T(2,128)(2,1)}, u32[]{:S(2)}, u32[]{:S(2)}) async-start(bf16[1024,2,1024]{2,1,0:T(2,128)(2,1)} %copy.36), calls=%async_computation.2 | async-start | bytes 8388608 | tf_op jit(solution)/shard_map/all_to_all | solution.py:50
  154.9 8.6 %fusion.8 = f32[2,512,1024]{2,1,0:T(8,128)} fusion(f32[2,512,1024]{2,1,0:T(8,128)} %param.8, bf16[1024,2,1024]{2,0,1:T(8,128)(2,1)} %all-gather.4.cloned.1.call-done, s32[]{:T(128)S(6)} %select_n.47), kind=kOutput, calls=%fused_computation.14 | convolution fusion | flops 2148532224 | bytes 14680068 | tf_op jit(solution)/shard_map/rjc,kjc->jrk/dot_general | solution.py:33
  163.5 4.5 %fusion.11 = f32[2,512,1024]{2,1,0:T(8,128)} fusion(f32[2,512,1024]{2,1,0:T(8,128)S(1)} %copy-done.2, bf16[1024,2,1024]{2,0,1:T(8,128)(2,1)S(1)} %copy-done.3, s32[]{:T(128)S(6)} %select_n.47), kind=kOutput, calls=%fused_computation.15 | convolution fusion | flops 2148532224 | bytes 14680068 | tf_op jit(solution)/shard_map/rjc,rjk->jck/dot_general | solution.py:37
  167.9 82.6 %all-to-all-done.1 = bf16[1024,2,1024]{2,1,0:T(2,128)(2,1)} async-done(((bf16[1024,2,1024]{2,1,0:T(2,128)(2,1)}), bf16[1024,2,1024]{2,1,0:T(2,128)(2,1)}, u32[]{:S(2)}, u32[]{:S(2)}) %all-to-all-start.1) | async-done | bytes 4194336 | tf_op jit(solution)/shard_map/all_to_all | solution.py:50
  250.5 3.5 %copy.37 = bf16[1024,2,1024]{2,0,1:T(8,128)(2,1)S(1)} copy(bf16[1024,2,1024]{2,1,0:T(2,128)(2,1)} %all-to-all-done.1) | data formatting | bytes 8388608 | tf_op jit(solution)/shard_map/all_to_all | solution.py:50
  254.0 2.4 copy.38
  256.4 4.9 %gather_fusion.1 = bf16[28,64,1024]{2,1,0:T(8,128)(2,1)} fusion(bf16[64,32,1024]{2,0,1:T(8,128)(2,1)} %bitcast.30, s32[1024]{0:T(1024)S(1)} %pad_clamp_fusion), kind=kCustom, calls=%fused_computation.1 | custom fusion | bytes 7340144 | tf_op jit(solution)/shard_map/jit(_take)/gather | solution.py:51
  261.2 2.6 copy.43
  263.8 2.6 broadcast_select_fusion
  (28 shorter events, 0.5 us)
Async XLA Ops:
  7.2 99.9 %copy-start = (bf16[2,512,1024]{2,1,0:T(8,128)(2,1)S(1)}, bf16[2,512,1024]{2,1,0:T(8,128)(2,1)}, u32[]{:S(2)}) copy-start(bf16[2,512,1024]{2,1,0:T(8,128)(2,1)} %param.10) | copy-start | bytes 6291460
  7.2 25.1 %reduce-scatter.2.cloned.1.call-start = ((), (), s32[]{:S(2)}) async-start(), calls=%async_computation.3 | async-start | bytes 5505024 | tf_op jit(solution)/shard_map/reduce_scatter | solution.py:25
  19.0 0.8 copy-start.4
  19.0 74.0 %all-gather.6.cloned.1.call-start = ((), (), s32[]{:S(2)}) async-start(), calls=%async_computation.5 | async-start | bytes 6291456 | tf_op jit(solution)/shard_map/all_gather | solution.py:32
  19.8 87.3 %all-gather.4.cloned.1.call-start = ((), (), s32[]{:S(2)}) async-start(), calls=%async_computation.4 | async-start | bytes 6291456 | tf_op jit(solution)/shard_map/all_gather | solution.py:30
  93.0 46.3 %all-gather.8.cloned.1.call-start = ((), (), s32[]{:S(2)}) async-start(), calls=%async_computation.6 | async-start | bytes 6291456 | tf_op jit(solution)/shard_map/all_gather | solution.py:49
  147.7 102.8 %all-to-all-start.1 = ((bf16[1024,2,1024]{2,1,0:T(2,128)(2,1)}), bf16[1024,2,1024]{2,1,0:T(2,128)(2,1)}, u32[]{:S(2)}, u32[]{:S(2)}) async-start(bf16[1024,2,1024]{2,1,0:T(2,128)(2,1)} %copy.36), calls=%async_computation.2 | async-start | bytes 8388608 | tf_op jit(solution)/shard_map/all_to_all | solution.py:50
  154.9 8.6 %copy-start.2 = (f32[2,512,1024]{2,1,0:T(8,128)S(1)}, f32[2,512,1024]{2,1,0:T(8,128)}, u32[]{:S(2)}) copy-start(f32[2,512,1024]{2,1,0:T(8,128)} %param.9) | copy-start | bytes 12582916
  154.9 8.6 %copy-start.3 = (bf16[1024,2,1024]{2,0,1:T(8,128)(2,1)S(1)}, bf16[1024,2,1024]{2,0,1:T(8,128)(2,1)}, u32[]{:S(2)}) copy-start(bf16[1024,2,1024]{2,0,1:T(8,128)(2,1)} %all-gather.4.cloned.1.call-done) | copy-start | bytes 12582916
  261.2 5.1 %copy-start.1 = (bf16[2,512,1024]{2,1,0:T(8,128)(2,1)S(1)}, bf16[2,512,1024]{2,1,0:T(8,128)(2,1)}, u32[]{:S(2)}) copy-start(bf16[2,512,1024]{2,1,0:T(8,128)(2,1)} %param.10) | copy-start | bytes 6291460
Sparse Core Ops, SparseCore 0:
  19.1 13.0 reduce-scatter.1
  33.8 14.8 all-gather.5
  93.1 13.8 all-gather.3
  124.4 14.8 all-gather.7
where the time goes:
time: 273 us
  waiting for transfers between devices  124 us (45%)
  blocking collectives  56.4 us (21%)
  local copies, waits for them, and re-layouts  38.6 us (14%)
  matrix products  23.5 us (9%)
  between operations  13.9 us (5%)
  other arithmetic  8.9 us (3%)
  starting transfers between devices  7.12 us (3%)
    all_to_all x1, waiting for transfers between devices, per_device(): lax.all_to_all(full_rows, 'fsdp', split_axis=0, concat_axis=1, tiled=True)  82.6 us
    all_to_all x1, blocking collectives, per_device(): lax.all_to_all(outgoing, 'fsdp', split_axis=1, concat_axis=0, tiled=True)  53.8 us
    all_gather x1, waiting for transfers between devices, per_device(): full_rows = lax.all_gather(scaled, 'dp', axis=0, tiled=True)  15 us
    all_gather x1, waiting for transfers between devices, per_device(): gradient = lax.all_gather(incoming, 'dp', axis=2, tiled=True)  14 us
    reduce_scatter x1, waiting for transfers between devices, per_device(): lax.psum_scatter(band.astype(jnp.bfloat16), 'dp', scatter_dimension=2, ti...  12.2 us
    squeeze x2, local copies, waits for them, and re-layouts, per_device(): local_rows = grads[0]  11.7 us
    dot_general x1, matrix products, per_device(): jnp.einsum('rjc,jck->rjk', left_applied, whole_right, preferred_element_t...  10.4 us
    dot_general x1, matrix products, per_device(): jnp.einsum('rjc,kjc->jrk', own_rows, gradient, preferred_element_type=jnp...  8.58 us
  transfers between devices with their start and end apart: 5, of which 4 were waited for; matrix products, arithmetic and copies ran while one was open for 7% of the time, Pallas kernels for 0%

commit v1 on v0

--- a/solution.py
+++ b/solution.py
@@ -47,7 +47,12 @@
     factor = lax.rsqrt(squares / (block_size * block_size) + epsilon)
     scaled = (both_applied * factor[None, :, None]).astype(jnp.bfloat16)
     full_rows = lax.all_gather(scaled, "dp", axis=0, tiled=True)
-    returned = lax.all_to_all(full_rows, "fsdp", split_axis=0, concat_axis=1, tiled=True)
+    returned = jnp.concatenate(
+        lax.all_to_all(
+            jnp.stack(jnp.split(full_rows, lax.axis_size("fsdp"), axis=0)), "fsdp", 0, 0
+        ),
+        axis=1,
+    )
     update = jnp.take(returned, block_slot, axis=1).reshape(row_dev, col_count)
     return (left_new, right_new, update)
 

time: 273 us -> 286 us (1.048)
  local copies, waits for them, and re-layouts: 38.6 us -> 51.1 us
    unnamed x10 -> x25, local copies, waits for them, and re-layouts: 0.03 us -> 25.1 us
    all_gather x1 -> x0, local copies, waits for them, and re-layouts: 8.48 us -> none  [per_device(): full_rows = lax.all_gather(scaled, 'dp', axis=0, tiled=True)]
    all_to_all x2 -> x0, local copies, waits for them, and re-layouts: 5.86 us -> none  [per_device(): lax.all_to_all(full_rows, 'fsdp', split_axis=0, concat_axis=1, tiled=True)]
    dot_general x1, matrix products: 8.58 us -> 4.4 us  [per_device(): jnp.einsum('rjc,kjc->jrk', own_rows, gradient, preferred_element_type=jnp...]
    dot_general x1, matrix products: 4.46 us -> 8.6 us  [per_device(): jnp.einsum('rjc,rjk->jck', columns, gradient, preferred_element_type=jnp....]
where the time goes in v1:
time: 286 us; the launch traced here: 285 us
  waiting for transfers between devices  125 us (44%)
  blocking collectives  56.2 us (20%)
  local copies, waits for them, and re-layouts  51.1 us (18%)
  matrix products  23.4 us (8%)
  between operations  13.9 us (5%)
  other arithmetic  8.9 us (3%)
  starting transfers between devices  7.12 us (2%)
    all_to_all x1, waiting for transfers between devices, per_device(): lax.all_to_all(jnp.stack(jnp.split(full_rows, lax.axis_size('fsdp'), axis...  82.6 us
    all_to_all x1, blocking collectives, per_device(): lax.all_to_all(outgoing, 'fsdp', split_axis=1, concat_axis=0, tiled=True)  53.8 us
    unnamed x25, local copies, waits for them, and re-layouts  25.1 us
    all_gather x1, waiting for transfers between devices, per_device(): full_rows = lax.all_gather(scaled, 'dp', axis=0, tiled=True)  15 us
    all_gather x1, waiting for transfers between devices, per_device(): gradient = lax.all_gather(incoming, 'dp', axis=2, tiled=True)  14 us
    reduce_scatter x1, waiting for transfers between devices, per_device(): lax.psum_scatter(band.astype(jnp.bfloat16), 'dp', scatter_dimension=2, ti...  12.2 us
    squeeze x2, local copies, waits for them, and re-layouts, per_device(): local_rows = grads[0]  11.7 us
    dot_general x1, matrix products, per_device(): jnp.einsum('rjc,jck->rjk', left_applied, whole_right, preferred_element_t...  10.4 us
  transfers between devices with their start and end apart: 5, of which 4 were waited for; matrix products, arithmetic and copies ran while one was open for 7% of the time, Pallas kernels for 0%

profile of v1, /device:TPU:14, one launch (start us, length us, event | category | flops | bytes accessed | tf_op | source)
XLA Modules:
  0.0 285.2 jit_solution(7871406676072884298)
XLA Ops:
  7.2 5.7 %squeeze.3 = bf16[64,28,1024]{2,1,0:T(8,128)(2,1)} reshape(bf16[1,64,28672]{2,1,0:T(8,128)(2,1)} %param.6) | data formatting | bytes 7340032 | tf_op jit(solution)/shard_map/squeeze | solution.py:10
  12.9 6.0 %copy.20 = bf16[64,28,1024]{2,0,1:T(8,128)(2,1)} copy(bf16[64,28,1024]{2,1,0:T(8,128)(2,1)} %squeeze.3) | data formatting | bytes 7340032 | tf_op jit(solution)/shard_map/squeeze | solution.py:10
  20.1 12.2 %reduce-scatter.2.cloned.1.call-done = bf16[64,28,512]{2,0,1:T(8,128)(2,1)} async-done(((bf16[64,28,1024]{2,0,1:T(8,128)(2,1)}), bf16[64,28,512]{2,0,1:T(8,128)(2,1)}) %reduce-scatter.2.cloned.1.call-update) | async-done | bytes 1835024 | tf_op jit(solution)/shard_map/reduce_scatter | solution.py:25
  32.3 3.5 %gather_fusion = bf16[32,64,512]{2,1,0:T(8,128)(2,1)} fusion(bf16[64,28,512]{2,0,1:T(8,128)(2,1)} %reduce-scatter.2.cloned.1.call-done, s32[1024]{0:T(1024)S(1)} %pad_clamp_fusion.1), kind=kCustom, calls=%fused_computation | custom fusion | bytes 4194432 | tf_op jit(solution)/shard_map/jit(_take)/gather | solution.py:27
  35.8 1.9 select_bitcast_fusion
  37.7 53.8 %all_to_all.23 = bf16[64,32,512]{2,0,1:T(8,128)(2,1)S(1)} all-to-all(bf16[64,32,512]{2,0,1:T(8,128)(2,1)S(1)} %select_bitcast_fusion), channel_id=1, replica_groups=mesh['fsdp'=16,'dp'=2] {'fsdp'}, dimensions={1} | all-to-all | bytes 4194304 | tf_op jit(solution)/shard_map/all_to_all | solution.py:29
  93.1 14.0 %all-gather.4.cloned.1.call-done = bf16[1024,2,1024]{2,0,1:T(8,128)(2,1)} async-done(((bf16[1024,2,512]{2,0,1:T(8,128)(2,1)}), bf16[1024,2,1024]{2,0,1:T(8,128)(2,1)}) %all-gather.4.cloned.1.call-update) | async-done | bytes 4194320 | tf_op jit(solution)/shard_map/all_gather | solution.py:30
  107.1 10.4 %multiply_reduce_fusion = (f32[2]{0:T(128)S(1)}, f32[2,512,1024]{2,1,0:T(8,128)}) fusion(bf16[2,1024,1024]{2,1,0:T(8,128)(2,1)} %all-gather.6.cloned.1.call-done, bf16[1024,2,1024]{2,0,1:T(8,128)(2,1)} %all-gather.4.cloned.1.call-done, bf16[2,512,1024]{2,1,0:T(8,128)(2,1)S(1)} %copy-done), kind=kOutput, calls=%fused_computation.3 | convolution fusion | flops 4298113024 | bytes 14680072 | tf_op jit(solution)/shard_map/rjc,jck->rjk/dot_general | solution.py:43
  117.5 2.4 psum.7
  120.0 4.1 %fusion = bf16[512,2,1024]{2,0,1:T(8,128)(2,1)} fusion(f32[2,512,1024]{2,1,0:T(8,128)} %get-tuple-element.4, f32[2]{0:T(128)S(1)} %add_rsqrt_fusion), kind=kLoop, calls=%fused_computation.5 | loop fusion | flops 2097152 | bytes 6291464 | tf_op jit(solution)/shard_map/convert_element_type | solution.py:48
  124.2 15.0 %all-gather.8.cloned.1.call-done = bf16[1024,2,1024]{2,0,1:T(8,128)(2,1)} async-done(((bf16[512,2,1024]{2,0,1:T(8,128)(2,1)}), bf16[1024,2,1024]{2,0,1:T(8,128)(2,1)}) %all-gather.8.cloned.1.call-update) | async-done | bytes 4194320 | tf_op jit(solution)/shard_map/all_gather | solution.py:49
  139.2 1.7 fusion.31
  140.9 1.7 fusion.30
  142.5 1.7 fusion.29
  144.2 1.7 fusion.28
  155.9 1.7 fusion.21
  157.6 1.7 fusion.20
  165.9 7.0 %all-to-all-start.1 = ((bf16[16,64,2,1024]{3,1,2,0:T(8,128)(2,1)}), bf16[16,64,2,1024]{3,1,2,0:T(8,128)(2,1)}, u32[]{:S(2)}, u32[]{:S(2)}) async-start(bf16[16,64,2,1024]{3,1,2,0:T(8,128)(2,1)} %fusion.16), calls=%async_computation.2 | async-start | bytes 8388608 | tf_op jit(solution)/shard_map/all_to_all | solution.py:51
  173.0 8.6 %fusion.11 = f32[2,512,1024]{2,1,0:T(8,128)} fusion(f32[2,512,1024]{2,1,0:T(8,128)} %param.9, bf16[1024,2,1024]{2,0,1:T(8,128)(2,1)} %all-gather.4.cloned.1.call-done, s32[]{:T(128)S(6)} %select_n.47), kind=kOutput, calls=%fused_computation.15 | convolution fusion | flops 2148532224 | bytes 14680068 | tf_op jit(solution)/shard_map/rjc,rjk->jck/dot_general | solution.py:37
  181.6 4.4 %fusion.8 = f32[2,512,1024]{2,1,0:T(8,128)} fusion(f32[2,512,1024]{2,1,0:T(8,128)S(1)} %copy-done.2, bf16[1024,2,1024]{2,0,1:T(8,128)(2,1)S(1)} %copy-done.3, s32[]{:T(128)S(6)} %select_n.47), kind=kOutput, calls=%fused_computation.14 | convolution fusion | flops 2148532224 | bytes 14680068 | tf_op jit(solution)/shard_map/rjc,kjc->jrk/dot_general | solution.py:33
  186.0 82.6 %all-to-all-done.1 = bf16[16,64,2,1024]{3,1,2,0:T(8,128)(2,1)} async-done(((bf16[16,64,2,1024]{3,1,2,0:T(8,128)(2,1)}), bf16[16,64,2,1024]{3,1,2,0:T(8,128)(2,1)}, u32[]{:S(2)}, u32[]{:S(2)}) %all-to-all-start.1) | async-done | bytes 4194336 | tf_op jit(solution)/shard_map/all_to_all | solution.py:51
  268.6 4.9 %gather_fusion.1 = bf16[28,64,1024]{2,1,0:T(8,128)(2,1)} fusion(bf16[64,32,1024]{2,0,1:T(8,128)(2,1)} %bitcast.25, s32[1024]{0:T(1024)S(1)} %pad_clamp_fusion), kind=kCustom, calls=%fused_computation.1 | custom fusion | bytes 7340144 | tf_op jit(solution)/shard_map/jit(_take)/gather | solution.py:56
  273.5 2.6 copy.29
  276.1 2.6 broadcast_select_fusion
  (41 shorter events, 19.5 us)
Async XLA Ops:
  7.2 100.0 %copy-start = (bf16[2,512,1024]{2,1,0:T(8,128)(2,1)S(1)}, bf16[2,512,1024]{2,1,0:T(8,128)(2,1)}, u32[]{:S(2)}) copy-start(bf16[2,512,1024]{2,1,0:T(8,128)(2,1)} %param.10) | copy-start | bytes 6291460
  7.2 25.1 %reduce-scatter.2.cloned.1.call-start = ((), (), s32[]{:S(2)}) async-start(), calls=%async_computation.3 | async-start | bytes 5505024 | tf_op jit(solution)/shard_map/reduce_scatter | solution.py:25
  19.0 0.8 copy-start.4
  19.0 74.1 %all-gather.6.cloned.1.call-start = ((), (), s32[]{:S(2)}) async-start(), calls=%async_computation.5 | async-start | bytes 6291456 | tf_op jit(solution)/shard_map/all_gather | solution.py:32
  19.8 87.4 %all-gather.4.cloned.1.call-start = ((), (), s32[]{:S(2)}) async-start(), calls=%async_computation.4 | async-start | bytes 6291456 | tf_op jit(solution)/shard_map/all_gather | solution.py:30
  93.1 46.1 %all-gather.8.cloned.1.call-start = ((), (), s32[]{:S(2)}) async-start(), calls=%async_computation.6 | async-start | bytes 6291456 | tf_op jit(solution)/shard_map/all_gather | solution.py:49
  165.9 102.8 %all-to-all-start.1 = ((bf16[16,64,2,1024]{3,1,2,0:T(8,128)(2,1)}), bf16[16,64,2,1024]{3,1,2,0:T(8,128)(2,1)}, u32[]{:S(2)}, u32[]{:S(2)}) async-start(bf16[16,64,2,1024]{3,1,2,0:T(8,128)(2,1)} %fusion.16), calls=%async_computation.2 | async-start | bytes 8388608 | tf_op jit(solution)/shard_map/all_to_all | solution.py:51
  173.0 8.6 %copy-start.2 = (f32[2,512,1024]{2,1,0:T(8,128)S(1)}, f32[2,512,1024]{2,1,0:T(8,128)}, u32[]{:S(2)}) copy-start(f32[2,512,1024]{2,1,0:T(8,128)} %param.8) | copy-start | bytes 12582916
  173.0 8.6 %copy-start.3 = (bf16[1024,2,1024]{2,0,1:T(8,128)(2,1)S(1)}, bf16[1024,2,1024]{2,0,1:T(8,128)(2,1)}, u32[]{:S(2)}) copy-start(bf16[1024,2,1024]{2,0,1:T(8,128)(2,1)} %all-gather.4.cloned.1.call-done) | copy-start | bytes 12582916
  273.5 5.1 %copy-start.1 = (bf16[2,512,1024]{2,1,0:T(8,128)(2,1)S(1)}, bf16[2,512,1024]{2,1,0:T(8,128)(2,1)}, u32[]{:S(2)}) copy-start(bf16[2,512,1024]{2,1,0:T(8,128)(2,1)} %param.10) | copy-start | bytes 6291460
Sparse Core Ops, SparseCore 0:
  19.1 13.0 reduce-scatter.1
  33.8 14.8 all-gather.5
  93.2 13.8 all-gather.3
  124.3 14.8 all-gather.7
